TPU v7x, 32 devices: a whole 2x2x4 slice. The times are simulated.
32 devices in a mesh: groups: 2 (over y), shard: 16 (over z, x, core).
Axes of the slice: x: 2, y: 2, z: 4, core: 2. Of those that a mesh axis runs over, the one named last changes fastest.
Arguments:
- grad_out: bfloat16 [4, 4096, 2048], P('groups', 'shard'), parts along dimension 0, may hold values from -6 to 6
- saved_input: bfloat16 [4, 4096, 2048], P('groups', 'shard'), parts along dimension 0, may hold values from -6 to 6
- lengths: int32 [4], P('groups'), parts along dimension 0, may hold values from 1024 to 4096, as said below
- kernel: float32 [31, 2048], replicated, may hold values from -1 to 1
- gain: float32 [2048], replicated, may hold values from 0.1 to 1.9
- bias: float32 [2048], replicated, may hold values from -4 to 4
- proj_weight: bfloat16 [2048, 2048], P('shard'), may hold values from -0.125 to 0.125
Outputs:
- input_grad: bfloat16 [4, 4096, 2048], P('groups', 'shard'), parts along dimension 0
- proj_grad: float32 [4096, 2048], P(('groups', 'shard')), parts along dimension 0
- kernel_grad: float32 [62, 2048], P('groups', 'shard'), parts along dimension 0
- norm_grads: float32 [4, 2048], P('groups', 'shard'), parts along dimension 0
There are 2 independent parts, one for each index of `groups`. A program takes and returns all parts, laid end to end along the dimension named above; an argument that names none is the same for every part. Nothing has to cross between parts.
Inputs may be any that keep to these rules, and one draw needn't show every extreme that they name: `lengths`: one utterance of every microbatch is live over all 4096 frames.
All inputs are finite; a program needn't handle non-finite values.
Results may differ from a plain program's by a relative error of at most 0.0051.
Values may be sent and summed in bfloat16 or wider, within the bound.
No kernel may reach another device: no remote copies, remote signals or barrier semaphores. Data moves between devices by JAX's collectives and lax.ppermute only.
A program may use at most 128 MiB of HBM per device.

v0:
```python
import jax
import jax.numpy as jnp
from jax import lax
from jax.sharding import PartitionSpec as P


def extended(block, sides, width):
    for axis, dim in sides:
        count = lax.axis_size(axis)
        forward = [(i, i + 1) for i in range(count - 1)]
        backward = [(target, source) for source, target in forward]
        low = lax.ppermute(
            lax.slice_in_dim(block, block.shape[dim] - width, None, axis=dim), axis, forward
        )
        high = lax.ppermute(lax.slice_in_dim(block, 0, width, axis=dim), axis, backward)
        block = jnp.concatenate([low, block, high], axis=dim)
    return block


def frame_mask(lengths, offset, count):
    position = offset + jnp.arange(count, dtype=jnp.int32)
    return (position[None, :] < lengths[:, None])[:, :, None]


def forward_taps(padded, kernel, count):
    total = jnp.zeros((padded.shape[0], count, padded.shape[2]), jnp.float32)
    for index_tap in range(kernel.shape[0]):
        total = total + kernel[index_tap] * padded[:, index_tap : index_tap + count, :].astype(
            jnp.float32
        )
    return total


def backward_taps(padded, kernel, count, half_span):
    total = jnp.zeros((padded.shape[0], count, padded.shape[2]), jnp.float32)
    for index_tap in range(kernel.shape[0]):
        begin = 2 * half_span - index_tap
        total = total + kernel[index_tap] * padded[:, begin : begin + count, :].astype(jnp.float32)
    return total


def pre_gradient(act_grad, pre_act, gate_sig):
    return act_grad * gate_sig * (1.0 + pre_act * (1.0 - gate_sig))


def shards(grad_out, saved_input, lengths, kernel, gain, bias, proj_weight):
    batches, frames, model_width = grad_out.shape
    tap_count = kernel.shape[0]
    half_span = (tap_count - 1) // 2
    offset = lax.axis_index("shard") * frames
    norm_scale = lax.rsqrt(jnp.sum(lengths).astype(jnp.float32))
    own_mask = frame_mask(lengths, offset, frames)
    masked_in = jnp.where(own_mask, saved_input, jnp.zeros_like(saved_input))
    masked_grad = jnp.where(own_mask, grad_out, jnp.zeros_like(grad_out))
    in_ext = extended(masked_in, (("shard", 1),), half_span)
    conv = forward_taps(in_ext, kernel, frames)
    pre_act = gain * conv + bias
    gate_sig = jax.nn.sigmoid(pre_act)
    activated = (pre_act * gate_sig).astype(jnp.bfloat16)
    rows = masked_grad.reshape(batches * frames, model_width)
    act_grad = lax.dot_general(
        rows,
        lax.all_gather(proj_weight, "shard", axis=0, tiled=True),
        (((1,), (1,)), ((), ())),
        preferred_element_type=jnp.float32,
    )
    act_grad = act_grad.reshape(batches, frames, model_width)
    pre_grad = pre_gradient(act_grad, pre_act, gate_sig)
    conv_grad = (pre_grad * gain).astype(jnp.bfloat16)
    grad_ext = extended(conv_grad, (("shard", 1),), half_span)
    back_sum = backward_taps(grad_ext, kernel, frames, half_span)
    input_grad = jnp.where(own_mask, back_sum, jnp.zeros_like(back_sum)).astype(jnp.bfloat16)
    grad_float = conv_grad.astype(jnp.float32)
    tap_rows = []
    for index_tap in range(tap_count):
        tap_rows.append(
            jnp.sum(
                in_ext[:, index_tap : index_tap + frames, :].astype(jnp.float32) * grad_float,
                axis=(0, 1),
            )
        )
    gain_term = jnp.sum(pre_grad * conv, axis=(0, 1))
    bias_term = jnp.sum(pre_grad, axis=(0, 1))
    stats = (
        jnp.concatenate([jnp.stack(tap_rows, 0), gain_term[None, :], bias_term[None, :]], 0)
        * norm_scale
    )
    summed = lax.psum_scatter(stats, "shard", scatter_dimension=1, tiled=True)
    act_flat = activated.reshape(batches * frames, model_width)
    grad_flat = masked_grad.reshape(batches * frames, model_width)
    product = lax.dot_general(
        act_flat, grad_flat, (((0,), (0,)), ((), ())), preferred_element_type=jnp.float32
    )
    proj_grad = lax.psum_scatter(product * norm_scale, "shard", scatter_dimension=0, tiled=True)
    return (input_grad, proj_grad, summed[:tap_count], summed[tap_count:])


def solution(mesh):
    placed = (
        P("groups", "shard", None),
        P("groups", "shard", None),
        P("groups"),
        P(),
        P(),
        P(),
        P("shard", None),
    )
    return jax.shard_map(
        shards,
        mesh=mesh,
        in_specs=placed,
        out_specs=(
            P("groups", "shard", None),
            P(("groups", "shard"), None),
            P("groups", "shard"),
            P("groups", "shard"),
        ),
        check_vma=False,
    )
```

profile of v0, /device:TPU:0, one launch (start us, length us, event | category | flops | bytes accessed | tf_op | source)
XLA Modules:
  0.0 358.8 jit_solution(6683365400777504485)
XLA Ops:
  7.2 0.0 copy-start.4
  7.2 0.0 copy-start.3
  7.2 0.0 all-gather.2.cloned.1.call-start
  7.2 0.7 all-gather.2.cloned.1.call-update
  7.9 0.0 reduce-scatter.5.cloned.1.call-start
  8.0 0.7 broadcast_compare_fusion
  8.7 1.8 broadcast_select_fusion
  10.5 0.0 copy-start.5
  10.5 0.0 copy-start.6
  10.6 2.4 collective-permute-start
  13.0 1.3 collective-permute-start.1
  14.3 0.0 copy-done.3
  14.3 0.1 fusion.148
  14.4 0.1 fusion.149
  14.5 0.0 copy-done.4
  14.5 0.6 reduce_sum.306
  15.8 0.0 collective-permute-done
  15.9 2.5 collective-permute-done.1
  18.3 19.8 %fusion.31 = f32[2,256,2048]{2,1,0:T(8,128)} fusion(bf16[2,256,2048]{2,1,0:T(8,128)(2,1)S(1)} %broadcast_select_fusion, bf16[2,15,2048]{2,1,0:T(8,128)(2,1)S(1)} %collective-permute-done.1, bf16[2,15,2048]{2,1,0:T(8,128)(2,1)S(1)} %collective-permute-done, f32[2048]{0:T(1024)S(1)} %bitcast.131, f32[2048]{0:T(1024)S(1)} %bitcast.133, f32[2048]{0:T(1024)S(1)} %bitcast.75, ...), kind=kLoop, calls=%fused_computation.151 | loop fusion | flops 190840832 | bytes 6791168 | tf_op jit(solution)/shard_map/add | solution.py:28
  38.2 49.0 %all-gather.2.cloned.1.call-done = bf16[2048,2048]{1,0:T(8,128)(2,1)} async-done(((bf16[128,2048]{1,0:T(8,128)(2,1)}), bf16[2048,2048]{1,0:T(8,128)(2,1)}) %all-gather.2.cloned.1.call-update) | async-done | bytes 8388624 | tf_op jit(solution)/shard_map/all_gather | solution.py:63
  87.2 0.0 copy-done.5
  87.2 0.0 copy-done.6
  87.2 0.0 copy-start.2
  87.2 16.0 %fusion.78 = (f32[2048]{0:T(1024)S(1)}, f32[2048]{0:T(1024)S(1)}, f32[2048]{0:T(1024)S(1)}, f32[2048]{0:T(1024)S(1)}, f32[2048]{0:T(1024)S(1)}, /*index=5*/f32[2...) fusion(bf16[2,15,2048]{2,1,0:T(8,128)(2,1)S(1)} %collective-per, ...), kind=kOutput, calls=%fused_computation.198 | convolution fusion | flops 4366252032 | bytes 23282176 | tf_op jit(solution)/shard_map/dot_general | solution.py:61
  103.2 0.0 copy-start
  103.2 0.0 copy-done.2
  103.3 1.2 fusion.145
  104.4 5.0 %fusion.77 = (f32[2048]{0:T(1024)S(1)}, f32[2048]{0:T(1024)S(1)}, f32[2048]{0:T(1024)S(1)}, f32[2048]{0:T(1024)S(1)}, f32[2048]{0:T(1024)S(1)}, /*index=5*/f32[2048]{0:T(1024)S(1)}, f32[2048]{0:T(1024)S(1)}) fusion(bf16[2,256,2048]{2,1,0:T(8,128)(2,1)S(1)} %get-tuple-element.37, bf16[2,15,2048]{2,1,0:T(8,128)(2,1)S(1)} %collective-permute-done.1, ...), kind=kLoop, calls=%fused_computation.197 | loop fusion | flops 41928704 | bytes 4374528 | tf_op jit(solution)/shard_map/reduce_sum | solution.py:77
  109.5 3.9 %fusion.61 = (f32[2048]{0:T(1024)S(1)}, f32[2048]{0:T(1024)S(1)}, f32[2048]{0:T(1024)S(1)}, f32[2048]{0:T(1024)S(1)}, f32[2048]{0:T(1024)S(1)}, /*index=5*/f32[2048]{0:T(1024)S(1)}) fusion(bf16[2,256,2048]{2,1,0:T(8,128)(2,1)S(1)} %get-tuple-element.37, bf16[2,256,2048]{2,1,0:T(8,128)(2,1)S(1)} %broadcast_select_fusion, ...), kind=kLoop, calls=%fused_computation.181 | loop fusion | flops 38785024 | bytes 4366336 | tf_op jit(solution)/shard_map/reduce_sum | solution.py:77
  113.4 0.0 copy-done
  113.4 5.4 %fusion.62 = (f32[2048]{0:T(1024)S(1)}, f32[2048]{0:T(1024)S(1)}, f32[2048]{0:T(1024)S(1)}, f32[2048]{0:T(1024)S(1)}, f32[2048]{0:T(1024)S(1)}, /*index=5*/f32[2...) fusion(bf16[2,256,2048]{2,1,0:T(8,128)(2,1)S(1)} %get-tuple-element.37, ...), kind=kLoop, calls=%fused_computation.182 | loop fusion | flops 57653248 | bytes 4390912 | tf_op jit(solution)/shard_map/reduce_sum | solution.py:77
  118.8 0.4 concatenate.77
  119.3 0.8 broadcast_multiply_fusion
  120.0 0.0 reduce-scatter.5.cloned.1.call-update
  120.0 0.2 reduce-scatter.3.cloned.1.call-start
  120.3 13.6 %bitcast_multiply_fusion = f32[2048,2048]{1,0:T(8,128)} fusion(f32[]{:T(128)S(6)} %rsqrt.3, f32[2,256,2048]{2,1,0:T(8,128)} %fusion.31, f32[2048]{0:T(1024)S(1)} %copy-done.6, f32[2048]{0:T(1024)S(1)} %copy-done.5, bf16[2,256,2048]{2,1,0:T(8,128)(2,1)} %param.7, pred[2,256]{1,0:T(4,128)(4,1)S(1)} %broadcast_compare_fusion), kind=kOutput, calls=%fused_computation.32 | convolution fusion | flops 4307550208 | bytes 23085572 | tf_op jit(solution)/shard_map/dot_general | solution.py:91
  133.8 0.0 copy-start.1
  133.9 0.0 reduce-scatter.3.cloned.1.call-update
  133.9 1.6 copy-done.1
  135.5 1.3 collective-permute-start.2
  136.8 3.0 collective-permute-start.3
  139.8 0.0 collective-permute-done.2
  139.8 1.0 collective-permute-done.3
  140.8 32.7 %select_convert_fusion = bf16[2,256,2048]{2,1,0:T(8,128)(2,1)} fusion(bf16[2,256,2048]{2,1,0:T(8,128)(2,1)S(1)} %copy-done.1, bf16[2,15,2048]{2,1,0:T(8,128)(2,1)S(1)} %collective-permute-done.3, bf16[2,15,2048]{2,1,0:T(8,128)(2,1)S(1)} %collective-permute-done.2, f32[2048]{0:T(1024)S(1)} %bitcast.132, f32[2048]{0:T(1024)S(1)} %bitcast.134, ...), kind=kLoop, calls=%fused_computation.201 | loop fusion | flops 192937984 | bytes 4694528 | tf_op jit(solution)/shard_map/convert_element_type | solution.py:72
  173.5 0.0 reduce-scatter.5.cloned.1.call-done
  173.5 1.3 slice.626
  174.8 1.3 slice.625
  176.1 176.2 %reduce-scatter.3.cloned.1.call-done = f32[128,2048]{1,0:T(8,128)} async-done(((f32[2048,2048]{1,0:T(8,128)}), f32[128,2048]{1,0:T(8,128)}) %reduce-scatter.3.cloned.1.call-update) | async-done | bytes 1048592 | tf_op jit(solution)/shard_map/reduce_scatter | solution.py:94
  (3 shorter events, 0.1 us)
Async XLA Ops:
  7.2 7.3 %copy-start.4 = (s32[2]{0:T(128)S(1)}, s32[2]{0:T(128)}, u32[]{:S(2)}) copy-start(s32[2]{0:T(128)} %param.9) | copy-start | bytes 28
  7.2 7.1 %copy-start.3 = (f32[31,2048]{1,0:T(8,128)S(1)}, f32[31,2048]{1,0:T(8,128)}, u32[]{:S(2)}) copy-start(f32[31,2048]{1,0:T(8,128)} %param.10) | copy-start | bytes 761860
  7.2 80.0 %all-gather.2.cloned.1.call-start = ((), (), s32[]{:S(2)}) async-start(), calls=%async_computation.2 | async-start | bytes 8912896 | tf_op jit(solution)/shard_map/all_gather | solution.py:63
  7.9 165.6 %reduce-scatter.5.cloned.1.call-start = ((), (), s32[]{:S(2)}) async-start(), calls=%async_computation.4 | async-start | bytes 348160 | tf_op jit(solution)/shard_map/reduce_scatter | solution.py:88
  10.5 76.7 %copy-start.5 = (f32[2048]{0:T(1024)S(1)}, f32[2048]{0:T(1024)}, u32[]{:S(2)}) copy-start(f32[2048]{0:T(1024)} %param.11) | copy-start | bytes 24580
  10.5 76.7 %copy-start.6 = (f32[2048]{0:T(1024)S(1)}, f32[2048]{0:T(1024)}, u32[]{:S(2)}) copy-start(f32[2048]{0:T(1024)} %param.12) | copy-start | bytes 24580
  10.6 5.3 %collective-permute-start = (bf16[2,15,2048]{2,1,0:T(8,128)(2,1)S(1)}, bf16[2,15,2048]{2,1,0:T(8,128)(2,1)S(1)}, u32[]{:S(2)}, u32[]{:S(2)}) collective-permute-start(bf16[2,15,2048]{2,1,0:T(8,128)(2,1)S(1)} %get-tuple-element.40), channel_id=1, source_target_pairs={{0,1},{1,2},{2,3},{3,4},{4,5},{5,6},{6,7},{7,8},{8,9},{9,10},{10,1... | collective-permute-start | bytes 368648 | tf_op jit(solution)/shard_map/ppermute | solution.py:12
  13.0 5.3 %collective-permute-start.1 = (bf16[2,15,2048]{2,1,0:T(8,128)(2,1)S(1)}, bf16[2,15,2048]{2,1,0:T(8,128)(2,1)S(1)}, u32[]{:S(2)}, u32[]{:S(2)}) collective-permute-start(bf16[2,15,2048]{2,1,0:T(8,128)(2,1)S(1)} %get-tuple-element.41), channel_id=1, source_target_pairs={{1,0},{2,1},{3,2},{4,3},{5,4},{6,5},{7,6},{8,7},{9,8},{10,9},{11,1... | collective-permute-start | bytes 368648 | tf_op jit(solution)/shard_map/ppermute | solution.py:15
  87.2 16.0 %copy-start.2 = (f32[2,256,2048]{2,1,0:T(8,128)S(1)}, f32[2,256,2048]{2,1,0:T(8,128)}, u32[]{:S(2)}) copy-start(f32[2,256,2048]{2,1,0:T(8,128)} %fusion.31) | copy-start | bytes 12582916
  103.2 10.1 %copy-start = (bf16[2,256,2048]{2,1,0:T(8,128)(2,1)}, bf16[2,256,2048]{2,1,0:T(8,128)(2,1)S(1)}, u32[]{:S(2)}) copy-start(bf16[2,256,2048]{2,1,0:T(8,128)(2,1)S(1)} %get-tuple-element.37) | copy-start | bytes 6291460
  120.0 232.3 %reduce-scatter.3.cloned.1.call-start = ((), (), s32[]{:S(2)}) async-start(), calls=%async_computation.3 | async-start | bytes 17825792 | tf_op jit(solution)/shard_map/reduce_scatter | solution.py:94
  133.8 1.6 copy-start.1
  135.5 4.3 %collective-permute-start.2 = (bf16[2,15,2048]{2,1,0:T(8,128)(2,1)S(1)}, bf16[2,15,2048]{2,1,0:T(8,128)(2,1)S(1)}, u32[]{:S(2)}, u32[]{:S(2)}) collective-permute-start(bf16[2,15,2048]{2,1,0:T(8,128)(2,1)S(1)} %get-tuple-element.38), channel_id=1, source_target_pairs={{1,0},{2,1},{3,2},{4,3},{5,4},{6,5},{7,6},{8,7},{9,8},{10,9},{11,1... | collective-permute-start | bytes 368648 | tf_op jit(solution)/shard_map/ppermute | solution.py:15
  136.8 4.0 %collective-permute-start.3 = (bf16[2,15,2048]{2,1,0:T(8,128)(2,1)S(1)}, bf16[2,15,2048]{2,1,0:T(8,128)(2,1)S(1)}, u32[]{:S(2)}, u32[]{:S(2)}) collective-permute-start(bf16[2,15,2048]{2,1,0:T(8,128)(2,1)S(1)} %get-tuple-element.39), channel_id=1, source_target_pairs={{0,1},{1,2},{2,3},{3,4},{4,5},{5,6},{6,7},{7,8},{8,9},{9,10},{10,1... | collective-permute-start | bytes 368648 | tf_op jit(solution)/shard_map/ppermute | solution.py:12
Sparse Core Ops, SparseCore 0:
  10.2 77.0 all-gather.1
  120.2 50.9 reduce-scatter.4
  175.9 176.3 reduce-scatter.2
where the time goes:
time: 359 us
  waiting for transfers between devices  229 us (64%)
  other arithmetic  72 us (20%)
  matrix products  29.6 us (8%)
  between operations  14.6 us (4%)
  starting transfers between devices  8.32 us (2%)
  local copies, waits for them, and re-layouts  4.89 us (1%)
    reduce_scatter x1, waiting for transfers between devices, shards(): lax.psum_scatter(product * norm_scale, 'shard', scatter_dimension=0, tile...  176 us
    all_gather x1, waiting for transfers between devices, shards(): lax.all_gather(proj_weight, 'shard', axis=0, tiled=True)  49 us
    convert_element_type x1, other arithmetic, shards(): jnp.where(own_mask, back_sum, jnp.zeros_like(back_sum)).astype(jnp.bfloat16)  32.7 us
    add x1, other arithmetic, forward_taps(): total + kernel[index_tap] * padded[:, index_tap:index_tap + count, :].ast...  19.8 us
    dot_general x1, matrix products, shards(): lax.dot_general(rows, lax.all_gather(proj_weight, 'shard', axis=0, tiled=...  16 us
    reduce_sum x3, other arithmetic, shards(): jnp.sum(in_ext[:, index_tap:index_tap + frames, :].astype(jnp.float32) *...  14.4 us
    dot_general x1, matrix products, shards(): lax.dot_general(act_flat, grad_flat, (((0,), (0,)), ((), ())), preferred_...  13.6 us
  transfers between devices with their start and end apart: 7, of which 4 were waited for; matrix products, arithmetic and copies ran while one was open for 20% of the time, Pallas kernels for 0%

commit v1 on v0

--- a/solution.py
+++ b/solution.py
@@ -2,6 +2,27 @@
 import jax.numpy as jnp
 from jax import lax
 from jax.sharding import PartitionSpec as P
+
+
+def collect(x, axis, dim):
+    size, place, width = (lax.axis_size(axis), lax.axis_index(axis), x.shape[dim])
+    right = [(i, (i + 1) % size) for i in range(size)]
+    backward = [(i, (i - 1) % size) for i in range(size)]
+    out = jnp.zeros((*x.shape[:dim], size * width, *x.shape[dim + 1 :]), x.dtype)
+    out = lax.dynamic_update_slice_in_dim(out, x, place * width, axis=dim)
+    from_left = from_right = x
+    half = size // 2
+    for step in range(1, half + 1):
+        from_left = lax.ppermute(from_left, axis, right)
+        out = lax.dynamic_update_slice_in_dim(
+            out, from_left, (place - step) % size * width, axis=dim
+        )
+        if step < size - half:
+            from_right = lax.ppermute(from_right, axis, backward)
+            out = lax.dynamic_update_slice_in_dim(
+                out, from_right, (place + step) % size * width, axis=dim
+            )
+    return out
 
 
 def extended(block, sides, width):
@@ -60,7 +81,7 @@
     rows = masked_grad.reshape(batches * frames, model_width)
     act_grad = lax.dot_general(
         rows,
-        lax.all_gather(proj_weight, "shard", axis=0, tiled=True),
+        collect(proj_weight, "shard", 0),
         (((1,), (1,)), ((), ())),
         preferred_element_type=jnp.float32,
     )

time: 359 us -> 406 us (1.13)
  starting transfers between devices: 8.32 us -> 69.3 us
  waiting for transfers between devices: 229 us -> 184 us
  local copies, waits for them, and re-layouts: 4.89 us -> 32.9 us
    ppermute x0 -> x15, starting transfers between devices: none -> 53.4 us  [the longest x8 35.6 us: collect(): from_left = lax.ppermute(from_left, axis, right)]
    all_gather x1 -> x0, waiting for transfers between devices: 49 us -> none  [shards(): lax.all_gather(proj_weight, 'shard', axis=0, tiled=True)]
    dynamic_update_slice x0 -> x16, local copies, waits for them, and re-layouts: none -> 18.8 us  [the longest x8 9.93 us: collect(): lax.dynamic_update_slice_in_dim(out, from_left, (place - step) % size * w...]
    ppermute x2, starting transfers between devices: 5.44 us -> 13 us  [extended(): lax.ppermute(lax.slice_in_dim(block, block.shape[dim] - width, None, axis...]
    ppermute x0 -> x15, waiting for transfers between devices: none -> 6.77 us  [the longest x8 6.75 us: collect(): from_left = lax.ppermute(from_left, axis, right)]
    broadcast_in_dim x0 -> x1, local copies, waits for them, and re-layouts: none -> 4.29 us  [collect(): out = jnp.zeros((*x.shape[:dim], size * width, *x.shape[dim + 1:]), x.dtype)]
  transfers between devices with their start and end apart: 7 -> 21, of which waited for: 4 -> 7; matrix products, arithmetic and copies ran while one was open for 20% -> 25% of each run, Pallas kernels for 0% -> 0%
where the time goes in v1:
time: 406 us; the launch traced here: 405 us
  waiting for transfers between devices  184 us (45%)
  other arithmetic  75 us (18%)
  starting transfers between devices  69.3 us (17%)
  local copies, waits for them, and re-layouts  32.9 us (8%)
  matrix products  28 us (7%)
  between operations  15.7 us (4%)
    reduce_scatter x1, waiting for transfers between devices, shards(): lax.psum_scatter(product * norm_scale, 'shard', scatter_dimension=0, tile...  177 us
    ppermute x8, starting transfers between devices, collect(): from_left = lax.ppermute(from_left, axis, right)  35.6 us
    convert_element_type x1, other arithmetic, shards(): jnp.where(own_mask, back_sum, jnp.zeros_like(back_sum)).astype(jnp.bfloat16)  32.7 us
    add x1, other arithmetic, forward_taps(): total + kernel[index_tap] * padded[:, index_tap:index_tap + count, :].ast...  22.9 us
    ppermute x7, starting transfers between devices, collect(): from_right = lax.ppermute(from_right, axis, backward)  17.8 us
    dot_general x1, matrix products, shards(): lax.dot_general(rows, collect(proj_weight, 'shard', 0), (((1,), (1,)), ((...  14.5 us
    reduce_sum x3, other arithmetic, shards(): jnp.sum(in_ext[:, index_tap:index_tap + frames, :].astype(jnp.float32) *...  14.4 us
    dot_general x1, matrix products, shards(): lax.dot_general(act_flat, grad_flat, (((0,), (0,)), ((), ())), preferred_...  13.6 us
  transfers between devices with their start and end apart: 21, of which 7 were waited for; matrix products, arithmetic and copies ran while one was open for 25% of the time, Pallas kernels for 0%

profile of v1, /device:TPU:0, one launch (start us, length us, event | category | flops | bytes accessed | tf_op | source)
XLA Modules:
  0.0 405.3 jit_solution(15079625928451379297)
XLA Ops:
  7.8 5.0 %collective-permute-start.1 = (bf16[128,2048]{1,0:T(8,128)(2,1)}, bf16[128,2048]{1,0:T(8,128)(2,1)S(1)}, u32[]{:S(2)}, u32[]{:S(2)}) collective-permute-start(bf16[128,2048]{1,0:T(8,128)(2,1)} %param.13), channel_id=1, source_target_pairs={{0,15},{1,0},{2,1},{3,2},{4,3},{5,4},{6,5},{7,6},{8,7},{9,8},{10,9... | collective-permute-start | bytes 1572872 | tf_op jit(solution)/shard_map/ppermute | solution.py:21
  13.5 1.8 broadcast_select_fusion
  15.3 4.6 %collective-permute-done = bf16[128,2048]{1,0:T(8,128)(2,1)S(1)} collective-permute-done((bf16[128,2048]{1,0:T(8,128)(2,1)}, bf16[128,2048]{1,0:T(8,128)(2,1)S(1)}, u32[]{:S(2)}, u32[]{:S(2)}) %collective-permute-start) | collective-permute-done | bytes 524320 | tf_op jit(solution)/shard_map/ppermute | solution.py:16
  19.9 2.5 collective-permute-start.2
  23.1 4.3 %collective-permute-start.15 = (bf16[2,15,2048]{2,1,0:T(8,128)(2,1)}, bf16[2,15,2048]{2,1,0:T(8,128)(2,1)S(1)}, u32[]{:S(2)}, u32[]{:S(2)}) collective-permute-start(bf16[2,15,2048]{2,1,0:T(8,128)(2,1)} %get-tuple-element.40), channel_id=1, source_target_pairs={{0,1},{1,2},{2,3},{3,4},{4,5},{5,6},{6,7},{7,8},{8,9},{9,10},{10,1... | collective-permute-start | bytes 368648 | tf_op jit(solution)/shard_map/ppermute | solution.py:33
  27.4 1.3 collective-permute-start.16
  30.4 2.5 fusion.148
  32.9 3.7 collective-permute-start.3
  36.6 2.1 fusion.149
  38.7 4.3 %broadcast_in_dim.36 = bf16[2048,2048]{1,0:T(8,128)(2,1)} broadcast(bf16[]{:T(256)} %constant.96.clone.1), dimensions={} | broadcast | bytes 8388610 | tf_op jit(solution)/shard_map/broadcast_in_dim | solution.py:11
  43.0 0.8 constant_dynamic-update-slice_fusion.15
  43.8 4.5 %collective-permute-start.5 = (bf16[128,2048]{1,0:T(8,128)(2,1)}, bf16[128,2048]{1,0:T(8,128)(2,1)}, u32[]{:S(2)}, u32[]{:S(2)}) collective-permute-start(bf16[128,2048]{1,0:T(8,128)(2,1)} %collective-permute-done.3), channel_id=1, source_target_pairs={{0,15},{1,0},{2,1},{3,2},{4,3},{5,4},{6,5},{7,6},{8,7},{9,8},{10,9... | collective-permute-start | bytes 1572872 | tf_op jit(solution)/shard_map/ppermute | solution.py:21
  48.3 4.7 %collective-permute-start.6 = (bf16[128,2048]{1,0:T(8,128)(2,1)}, bf16[128,2048]{1,0:T(8,128)(2,1)}, u32[]{:S(2)}, u32[]{:S(2)}) collective-permute-start(bf16[128,2048]{1,0:T(8,128)(2,1)} %collective-permute-done.4), channel_id=1, source_target_pairs={{0,1},{1,2},{2,3},{3,4},{4,5},{5,6},{6,7},{7,8},{8,9},{9,10},{10,1... | collective-permute-start | bytes 1572872 | tf_op jit(solution)/shard_map/ppermute | solution.py:16
  53.0 22.9 %fusion.31 = f32[2,256,2048]{2,1,0:T(8,128)} fusion(bf16[2,256,2048]{2,1,0:T(8,128)(2,1)S(1)} %broadcast_select_fusion, bf16[2,15,2048]{2,1,0:T(8,128)(2,1)S(1)} %collective-permute-done.16, bf16[2,15,2048]{2,1,0:T(8,128)(2,1)S(1)} %collective-permute-done.15, f32[2048]{0:T(1024)} %bitcast.131, f32[2048]{0:T(1024)} %bitcast.133, f32[2048]{0:T(1024)S(1)} %bitcast.75, ...), kind=kLoop, calls=%fused_computation.151 | loop fusion | flops 190840832 | bytes 6791168 | tf_op jit(solution)/shard_map/add | solution.py:49
  75.9 0.9 constant_dynamic-update-slice_fusion.14
  76.8 0.9 constant_dynamic-update-slice_fusion.13
  77.6 2.5 collective-permute-start.8
  80.1 1.9 constant_dynamic-update-slice_fusion.12
  82.0 1.9 constant_dynamic-update-slice_fusion.11
  83.9 4.5 %collective-permute-start.9 = (bf16[128,2048]{1,0:T(8,128)(2,1)S(1)}, bf16[128,2048]{1,0:T(8,128)(2,1)S(1)}, u32[]{:S(2)}, u32[]{:S(2)}) collective-permute-start(bf16[128,2048]{1,0:T(8,128)(2,1)S(1)} %collective-permute-done.7), channel_id=1, source_target_pairs={{0,15},{1,0},{2,1},{3,2},{4,3},{5,4},{6,5},{7,6},{8,7},{9,8},{10,9... | collective-permute-start | bytes 1572872 | tf_op jit(solution)/shard_map/ppermute | solution.py:21
  88.4 1.9 constant_dynamic-update-slice_fusion.10
  90.3 5.9 %collective-permute-start.10 = (bf16[128,2048]{1,0:T(8,128)(2,1)S(1)}, bf16[128,2048]{1,0:T(8,128)(2,1)S(1)}, u32[]{:S(2)}, u32[]{:S(2)}) collective-permute-start(bf16[128,2048]{1,0:T(8,128)(2,1)S(1)} %collective-permute-done.8), channel_id=1, source_target_pairs={{0,1},{1,2},{2,3},{3,4},{4,5},{5,6},{6,7},{7,8},{8,9},{9,10},{10,1... | collective-permute-start | bytes 1572872 | tf_op jit(solution)/shard_map/ppermute | solution.py:16
  96.2 1.9 constant_dynamic-update-slice_fusion.9
  98.1 1.9 constant_dynamic-update-slice_fusion.8
  100.0 0.9 constant_dynamic-update-slice_fusion.7
  101.7 8.6 %collective-permute-start.12 = (bf16[128,2048]{1,0:T(8,128)(2,1)S(1)}, bf16[128,2048]{1,0:T(8,128)(2,1)S(1)}, u32[]{:S(2)}, u32[]{:S(2)}) collective-permute-start(bf16[128,2048]{1,0:T(8,128)(2,1)S(1)} %collective-permute-done.10), channel_id=1, source_target_pairs={{0,1},{1,2},{2,3},{3,4},{4,5},{5,6},{6,7},{7,8},{8,9},{9,10},{10,1... | collective-permute-start | bytes 1572872 | tf_op jit(solution)/shard_map/ppermute | solution.py:16
  110.3 0.9 constant_dynamic-update-slice_fusion.6
  111.1 0.8 constant_dynamic-update-slice_fusion.5
  112.0 0.8 constant_dynamic-update-slice_fusion.4
  113.5 11.0 %collective-permute-start.14 = (bf16[128,2048]{1,0:T(8,128)(2,1)S(1)}, bf16[128,2048]{1,0:T(8,128)(2,1)S(1)}, u32[]{:S(2)}, u32[]{:S(2)}) collective-permute-start(bf16[128,2048]{1,0:T(8,128)(2,1)S(1)} %collective-permute-done.12), channel_id=1, source_target_pairs={{0,1},{1,2},{2,3},{3,4},{4,5},{5,6},{6,7},{7,8},{8,9},{9,10},{10,1... | collective-permute-start | bytes 1572872 | tf_op jit(solution)/shard_map/ppermute | solution.py:16
  124.5 0.8 constant_dynamic-update-slice_fusion.3
  125.3 0.9 constant_dynamic-update-slice_fusion.2
  126.2 0.9 constant_dynamic-update-slice_fusion.1
  127.7 0.8 constant_dynamic-update-slice_fusion
  128.5 14.5 %fusion.78 = (f32[2048]{0:T(1024)S(1)}, f32[2048]{0:T(1024)S(1)}, f32[2048]{0:T(1024)S(1)}, f32[2048]{0:T(1024)S(1)}, f32[2048]{0:T(1024)S(1)}, /*index=5*/f32[2...) fusion(bf16[2,15,2048]{2,1,0:T(8,128)(2,1)S(1)} %collective-per, ...), kind=kOutput, calls=%fused_computation.198 | convolution fusion | flops 4366252032 | bytes 23282176 | tf_op jit(solution)/shard_map/dot_general | solution.py:82
  143.1 1.2 fusion.145
  144.2 5.4 %fusion.62 = (f32[2048]{0:T(1024)S(1)}, f32[2048]{0:T(1024)S(1)}, f32[2048]{0:T(1024)S(1)}, f32[2048]{0:T(1024)S(1)}, f32[2048]{0:T(1024)S(1)}, /*index=5*/f32[2...) fusion(bf16[2,256,2048]{2,1,0:T(8,128)(2,1)S(1)} %get-tuple-element.37, ...), kind=kLoop, calls=%fused_computation.182 | loop fusion | flops 57653248 | bytes 4390912 | tf_op jit(solution)/shard_map/reduce_sum | solution.py:98
  149.7 5.0 %fusion.77 = (f32[2048]{0:T(1024)S(1)}, f32[2048]{0:T(1024)S(1)}, f32[2048]{0:T(1024)S(1)}, f32[2048]{0:T(1024)S(1)}, f32[2048]{0:T(1024)S(1)}, /*index=5*/f32[2048]{0:T(1024)S(1)}, f32[2048]{0:T(1024)S(1)}) fusion(bf16[2,256,2048]{2,1,0:T(8,128)(2,1)S(1)} %get-tuple-element.37, bf16[2,15,2048]{2,1,0:T(8,128)(2,1)S(1)} %collective-permute-done.16, ...), kind=kLoop, calls=%fused_computation.197 | loop fusion | flops 41928704 | bytes 4374528 | tf_op jit(solution)/shard_map/reduce_sum | solution.py:98
  154.7 3.9 fusion.61
  160.1 13.6 %bitcast_multiply_fusion = f32[2048,2048]{1,0:T(8,128)} fusion(f32[]{:T(128)S(6)} %rsqrt.3, f32[2,256,2048]{2,1,0:T(8,128)} %fusion.31, f32[2048]{0:T(1024)S(1)} %copy-done.38, f32[2048]{0:T(1024)S(1)} %copy-done.37, bf16[2,256,2048]{2,1,0:T(8,128)(2,1)} %param.7, pred[2,256]{1,0:T(4,128)(4,1)S(1)} %copy-done.34), kind=kOutput, calls=%fused_computation.32 | convolution fusion | flops 4307550208 | bytes 23085572 | tf_op jit(solution)/shard_map/dot_general | solution.py:112
  174.0 1.3 copy-done.1
  175.3 1.3 collective-permute-start.17
  176.6 8.7 %collective-permute-start.18 = (bf16[2,15,2048]{2,1,0:T(8,128)(2,1)S(1)}, bf16[2,15,2048]{2,1,0:T(8,128)(2,1)S(1)}, u32[]{:S(2)}, u32[]{:S(2)}) collective-permute-start(bf16[2,15,2048]{2,1,0:T(8,128)(2,1)S(1)} %get-tuple-element.39), channel_id=1, source_target_pairs={{0,1},{1,2},{2,3},{3,4},{4,5},{5,6},{6,7},{7,8},{8,9},{9,10},{10,1... | collective-permute-start | bytes 368648 | tf_op jit(solution)/shard_map/ppermute | solution.py:33
  185.4 1.0 collective-permute-done.18
  186.6 32.7 %select_convert_fusion = bf16[2,256,2048]{2,1,0:T(8,128)(2,1)} fusion(bf16[2,256,2048]{2,1,0:T(8,128)(2,1)S(1)} %copy-done.1, bf16[2,15,2048]{2,1,0:T(8,128)(2,1)S(1)} %collective-permute-done.18, bf16[2,15,2048]{2,1,0:T(8,128)(2,1)S(1)} %collective-permute-done.17, f32[2048]{0:T(1024)S(1)} %bitcast.132, f32[2048]{0:T(1024)S(1)} %bitcast.134, ...), kind=kLoop, calls=%fused_computation.201 | loop fusion | flops 192937984 | bytes 4694528 | tf_op jit(solution)/shard_map/convert_element_type | solution.py:93
  219.3 1.3 slice.625
  220.6 1.3 slice.626
  221.9 176.6 %reduce-scatter.3.cloned.1.call-done = f32[128,2048]{1,0:T(8,128)} async-done(((f32[2048,2048]{1,0:T(8,128)}), f32[128,2048]{1,0:T(8,128)}) %reduce-scatter.3.cloned.1.call-update) | async-done | bytes 1048592 | tf_op jit(solution)/shard_map/reduce_scatter | solution.py:115
  (111 shorter events, 6.6 us)
Async XLA Ops:
  7.2 21.8 %copy-start.35 = (s32[2]{0:T(128)S(1)}, s32[2]{0:T(128)}, u32[]{:S(2)}) copy-start(s32[2]{0:T(128)} %param.9) | copy-start | bytes 28
  7.2 212.1 %reduce-scatter.5.cloned.1.call-start = ((), (), s32[]{:S(2)}) async-start(), calls=%async_computation.3 | async-start | bytes 348160 | tf_op jit(solution)/shard_map/reduce_scatter | solution.py:109
  7.2 12.7 %collective-permute-start = (bf16[128,2048]{1,0:T(8,128)(2,1)}, bf16[128,2048]{1,0:T(8,128)(2,1)S(1)}, u32[]{:S(2)}, u32[]{:S(2)}) collective-permute-start(bf16[128,2048]{1,0:T(8,128)(2,1)} %param.13), channel_id=1, source_target_pairs={{0,1},{1,2},{2,3},{3,4},{4,5},{5,6},{6,7},{7,8},{8,9},{9,10},{10,1... | collective-permute-start | bytes 1572872 | tf_op jit(solution)/shard_map/ppermute | solution.py:16
  7.8 25.1 %collective-permute-start.1 = (bf16[128,2048]{1,0:T(8,128)(2,1)}, bf16[128,2048]{1,0:T(8,128)(2,1)S(1)}, u32[]{:S(2)}, u32[]{:S(2)}) collective-permute-start(bf16[128,2048]{1,0:T(8,128)(2,1)} %param.13), channel_id=1, source_target_pairs={{0,15},{1,0},{2,1},{3,2},{4,3},{5,4},{6,5},{7,6},{8,7},{9,8},{10,9... | collective-permute-start | bytes 1572872 | tf_op jit(solution)/shard_map/ppermute | solution.py:21
  19.9 16.7 %collective-permute-start.2 = (bf16[128,2048]{1,0:T(8,128)(2,1)S(1)}, bf16[128,2048]{1,0:T(8,128)(2,1)}, u32[]{:S(2)}, u32[]{:S(2)}) collective-permute-start(bf16[128,2048]{1,0:T(8,128)(2,1)S(1)} %collective-permute-done), channel_id=1, source_target_pairs={{0,1},{1,2},{2,3},{3,4},{4,5},{5,6},{6,7},{7,8},{8,9},{9,10},{10,1... | collective-permute-start | bytes 1572872 | tf_op jit(solution)/shard_map/ppermute | solution.py:16
  23.1 29.9 %collective-permute-start.15 = (bf16[2,15,2048]{2,1,0:T(8,128)(2,1)}, bf16[2,15,2048]{2,1,0:T(8,128)(2,1)S(1)}, u32[]{:S(2)}, u32[]{:S(2)}) collective-permute-start(bf16[2,15,2048]{2,1,0:T(8,128)(2,1)} %get-tuple-element.40), channel_id=1, source_target_pairs={{0,1},{1,2},{2,3},{3,4},{4,5},{5,6},{6,7},{7,8},{8,9},{9,10},{10,1... | collective-permute-start | bytes 368648 | tf_op jit(solution)/shard_map/ppermute | solution.py:33
  27.4 25.6 %collective-permute-start.16 = (bf16[2,15,2048]{2,1,0:T(8,128)(2,1)S(1)}, bf16[2,15,2048]{2,1,0:T(8,128)(2,1)S(1)}, u32[]{:S(2)}, u32[]{:S(2)}) collective-permute-start(bf16[2,15,2048]{2,1,0:T(8,128)(2,1)S(1)} %get-tuple-element.41), channel_id=1, source_target_pairs={{1,0},{2,1},{3,2},{4,3},{5,4},{6,5},{7,6},{8,7},{9,8},{10,9},{11,1... | collective-permute-start | bytes 368648 | tf_op jit(solution)/shard_map/ppermute | solution.py:36
  32.9 10.9 %collective-permute-start.3 = (bf16[128,2048]{1,0:T(8,128)(2,1)S(1)}, bf16[128,2048]{1,0:T(8,128)(2,1)}, u32[]{:S(2)}, u32[]{:S(2)}) collective-permute-start(bf16[128,2048]{1,0:T(8,128)(2,1)S(1)} %collective-permute-done.1), channel_id=1, source_target_pairs={{0,15},{1,0},{2,1},{3,2},{4,3},{5,4},{6,5},{7,6},{8,7},{9,8},{10,9... | collective-permute-start | bytes 1572872 | tf_op jit(solution)/shard_map/ppermute | solution.py:21
  36.6 11.7 %collective-permute-start.4 = (bf16[128,2048]{1,0:T(8,128)(2,1)}, bf16[128,2048]{1,0:T(8,128)(2,1)}, u32[]{:S(2)}, u32[]{:S(2)}) collective-permute-start(bf16[128,2048]{1,0:T(8,128)(2,1)} %collective-permute-done.2), channel_id=1, source_target_pairs={{0,1},{1,2},{2,3},{3,4},{4,5},{5,6},{6,7},{7,8},{8,9},{9,10},{10,1... | collective-permute-start | bytes 1572872 | tf_op jit(solution)/shard_map/ppermute | solution.py:16
  43.8 33.0 %collective-permute-start.5 = (bf16[128,2048]{1,0:T(8,128)(2,1)}, bf16[128,2048]{1,0:T(8,128)(2,1)}, u32[]{:S(2)}, u32[]{:S(2)}) collective-permute-start(bf16[128,2048]{1,0:T(8,128)(2,1)} %collective-permute-done.3), channel_id=1, source_target_pairs={{0,15},{1,0},{2,1},{3,2},{4,3},{5,4},{6,5},{7,6},{8,7},{9,8},{10,9... | collective-permute-start | bytes 1572872 | tf_op jit(solution)/shard_map/ppermute | solution.py:21
  48.3 29.3 %collective-permute-start.6 = (bf16[128,2048]{1,0:T(8,128)(2,1)}, bf16[128,2048]{1,0:T(8,128)(2,1)}, u32[]{:S(2)}, u32[]{:S(2)}) collective-permute-start(bf16[128,2048]{1,0:T(8,128)(2,1)} %collective-permute-done.4), channel_id=1, source_target_pairs={{0,1},{1,2},{2,3},{3,4},{4,5},{5,6},{6,7},{7,8},{8,9},{9,10},{10,1... | collective-permute-start | bytes 1572872 | tf_op jit(solution)/shard_map/ppermute | solution.py:16
  76.8 7.1 %collective-permute-start.7 = (bf16[128,2048]{1,0:T(8,128)(2,1)}, bf16[128,2048]{1,0:T(8,128)(2,1)S(1)}, u32[]{:S(2)}, u32[]{:S(2)}) collective-permute-start(bf16[128,2048]{1,0:T(8,128)(2,1)} %collective-permute-done.5), channel_id=1, source_target_pairs={{0,15},{1,0},{2,1},{3,2},{4,3},{5,4},{6,5},{7,6},{8,7},{9,8},{10,9... | collective-permute-start | bytes 1572872 | tf_op jit(solution)/shard_map/ppermute | solution.py:21
  77.6 12.7 %collective-permute-start.8 = (bf16[128,2048]{1,0:T(8,128)(2,1)}, bf16[128,2048]{1,0:T(8,128)(2,1)S(1)}, u32[]{:S(2)}, u32[]{:S(2)}) collective-permute-start(bf16[128,2048]{1,0:T(8,128)(2,1)} %collective-permute-done.6), channel_id=1, source_target_pairs={{0,1},{1,2},{2,3},{3,4},{4,5},{5,6},{6,7},{7,8},{8,9},{9,10},{10,1... | collective-permute-start | bytes 1572872 | tf_op jit(solution)/shard_map/ppermute | solution.py:16
  83.9 16.1 %collective-permute-start.9 = (bf16[128,2048]{1,0:T(8,128)(2,1)S(1)}, bf16[128,2048]{1,0:T(8,128)(2,1)S(1)}, u32[]{:S(2)}, u32[]{:S(2)}) collective-permute-start(bf16[128,2048]{1,0:T(8,128)(2,1)S(1)} %collective-permute-done.7), channel_id=1, source_target_pairs={{0,15},{1,0},{2,1},{3,2},{4,3},{5,4},{6,5},{7,6},{8,7},{9,8},{10,9... | collective-permute-start | bytes 1572872 | tf_op jit(solution)/shard_map/ppermute | solution.py:21
  90.3 11.4 %collective-permute-start.10 = (bf16[128,2048]{1,0:T(8,128)(2,1)S(1)}, bf16[128,2048]{1,0:T(8,128)(2,1)S(1)}, u32[]{:S(2)}, u32[]{:S(2)}) collective-permute-start(bf16[128,2048]{1,0:T(8,128)(2,1)S(1)} %collective-permute-done.8), channel_id=1, source_target_pairs={{0,1},{1,2},{2,3},{3,4},{4,5},{5,6},{6,7},{7,8},{8,9},{9,10},{10,1... | collective-permute-start | bytes 1572872 | tf_op jit(solution)/shard_map/ppermute | solution.py:16
  99.9 28.6 %copy-start.2 = (f32[2,256,2048]{2,1,0:T(8,128)S(1)}, f32[2,256,2048]{2,1,0:T(8,128)}, u32[]{:S(2)}) copy-start(f32[2,256,2048]{2,1,0:T(8,128)} %fusion.31) | copy-start | bytes 12582916
  100.0 28.6 %copy-start.34 = (pred[2,256]{1,0:T(4,128)(4,1)S(1)}, pred[2,256]{1,0:T(4,128)(4,1)}, u32[]{:S(2)}) copy-start(pred[2,256]{1,0:T(4,128)(4,1)} %copy-done.33) | copy-start | bytes 1540
  100.0 28.6 %copy-start.36 = (bf16[2,256,2048]{2,1,0:T(8,128)(2,1)S(1)}, bf16[2,256,2048]{2,1,0:T(8,128)(2,1)}, u32[]{:S(2)}) copy-start(bf16[2,256,2048]{2,1,0:T(8,128)(2,1)} %param.7) | copy-start | bytes 6291460
  100.0 28.6 %copy-start.37 = (f32[2048]{0:T(1024)S(1)}, f32[2048]{0:T(1024)}, u32[]{:S(2)}) copy-start(f32[2048]{0:T(1024)} %param.11) | copy-start | bytes 24580
  100.0 28.6 %copy-start.38 = (f32[2048]{0:T(1024)S(1)}, f32[2048]{0:T(1024)}, u32[]{:S(2)}) copy-start(f32[2048]{0:T(1024)} %param.12) | copy-start | bytes 24580
  100.0 12.0 %collective-permute-start.11 = (bf16[128,2048]{1,0:T(8,128)(2,1)S(1)}, bf16[128,2048]{1,0:T(8,128)(2,1)S(1)}, u32[]{:S(2)}, u32[]{:S(2)}) collective-permute-start(bf16[128,2048]{1,0:T(8,128)(2,1)S(1)} %collective-permute-done.9), channel_id=1, source_target_pairs={{0,15},{1,0},{2,1},{3,2},{4,3},{5,4},{6,5},{7,6},{8,7},{9,8},{10,9... | collective-permute-start | bytes 1572872 | tf_op jit(solution)/shard_map/ppermute | solution.py:21
  101.7 11.8 %collective-permute-start.12 = (bf16[128,2048]{1,0:T(8,128)(2,1)S(1)}, bf16[128,2048]{1,0:T(8,128)(2,1)S(1)}, u32[]{:S(2)}, u32[]{:S(2)}) collective-permute-start(bf16[128,2048]{1,0:T(8,128)(2,1)S(1)} %collective-permute-done.10), channel_id=1, source_target_pairs={{0,1},{1,2},{2,3},{3,4},{4,5},{5,6},{6,7},{7,8},{8,9},{9,10},{10,1... | collective-permute-start | bytes 1572872 | tf_op jit(solution)/shard_map/ppermute | solution.py:16
  112.0 14.2 %collective-permute-start.13 = (bf16[128,2048]{1,0:T(8,128)(2,1)S(1)}, bf16[128,2048]{1,0:T(8,128)(2,1)S(1)}, u32[]{:S(2)}, u32[]{:S(2)}) collective-permute-start(bf16[128,2048]{1,0:T(8,128)(2,1)S(1)} %collective-permute-done.11), channel_id=1, source_target_pairs={{0,15},{1,0},{2,1},{3,2},{4,3},{5,4},{6,5},{7,6},{8,7},{9,8},{10,9... | collective-permute-start | bytes 1572872 | tf_op jit(solution)/shard_map/ppermute | solution.py:21
  113.5 14.2 %collective-permute-start.14 = (bf16[128,2048]{1,0:T(8,128)(2,1)S(1)}, bf16[128,2048]{1,0:T(8,128)(2,1)S(1)}, u32[]{:S(2)}, u32[]{:S(2)}) collective-permute-start(bf16[128,2048]{1,0:T(8,128)(2,1)S(1)} %collective-permute-done.12), channel_id=1, source_target_pairs={{0,1},{1,2},{2,3},{3,4},{4,5},{5,6},{6,7},{7,8},{8,9},{9,10},{10,1... | collective-permute-start | bytes 1572872 | tf_op jit(solution)/shard_map/ppermute | solution.py:16
  159.9 238.6 %reduce-scatter.3.cloned.1.call-start = ((), (), s32[]{:S(2)}) async-start(), calls=%async_computation.2 | async-start | bytes 17825792 | tf_op jit(solution)/shard_map/reduce_scatter | solution.py:115
  173.7 12.7 %copy-start.4 = (f32[1,2048]{1,0:T(1,128)S(1)}, f32[1,2048]{1,0:T(1,128)}, u32[]{:S(2)}) copy-start(f32[1,2048]{1,0:T(1,128)} %get-tuple-element.44) | copy-start | bytes 24580
  173.7 12.7 %copy-start.5 = (f32[1,2048]{1,0:T(1,128)S(1)}, f32[1,2048]{1,0:T(1,128)}, u32[]{:S(2)}) copy-start(f32[1,2048]{1,0:T(1,128)} %get-tuple-element.45) | copy-start | bytes 24580
  173.7 12.7 %copy-start.6 = (f32[1,2048]{1,0:T(1,128)S(1)}, f32[1,2048]{1,0:T(1,128)}, u32[]{:S(2)}) copy-start(f32[1,2048]{1,0:T(1,128)} %get-tuple-element.46) | copy-start | bytes 24580
  173.7 12.7 %copy-start.7 = (f32[1,2048]{1,0:T(1,128)S(1)}, f32[1,2048]{1,0:T(1,128)}, u32[]{:S(2)}) copy-start(f32[1,2048]{1,0:T(1,128)} %get-tuple-element.47) | copy-start | bytes 24580
  173.7 12.7 %copy-start.8 = (f32[1,2048]{1,0:T(1,128)S(1)}, f32[1,2048]{1,0:T(1,128)}, u32[]{:S(2)}) copy-start(f32[1,2048]{1,0:T(1,128)} %get-tuple-element.48) | copy-start | bytes 24580
  173.7 12.7 %copy-start.9 = (f32[1,2048]{1,0:T(1,128)S(1)}, f32[1,2048]{1,0:T(1,128)}, u32[]{:S(2)}) copy-start(f32[1,2048]{1,0:T(1,128)} %get-tuple-element.49) | copy-start | bytes 24580
  173.7 12.7 %copy-start.10 = (f32[1,2048]{1,0:T(1,128)S(1)}, f32[1,2048]{1,0:T(1,128)}, u32[]{:S(2)}) copy-start(f32[1,2048]{1,0:T(1,128)} %get-tuple-element.50) | copy-start | bytes 24580
  173.7 12.7 %copy-start.11 = (f32[1,2048]{1,0:T(1,128)S(1)}, f32[1,2048]{1,0:T(1,128)}, u32[]{:S(2)}) copy-start(f32[1,2048]{1,0:T(1,128)} %get-tuple-element.51) | copy-start | bytes 24580
  173.8 12.7 %copy-start.12 = (f32[1,2048]{1,0:T(1,128)S(1)}, f32[1,2048]{1,0:T(1,128)}, u32[]{:S(2)}) copy-start(f32[1,2048]{1,0:T(1,128)} %get-tuple-element.52) | copy-start | bytes 24580
  173.8 12.7 %copy-start.13 = (f32[1,2048]{1,0:T(1,128)S(1)}, f32[1,2048]{1,0:T(1,128)}, u32[]{:S(2)}) copy-start(f32[1,2048]{1,0:T(1,128)} %get-tuple-element.53) | copy-start | bytes 24580
  173.8 12.7 %copy-start.14 = (f32[1,2048]{1,0:T(1,128)S(1)}, f32[1,2048]{1,0:T(1,128)}, u32[]{:S(2)}) copy-start(f32[1,2048]{1,0:T(1,128)} %get-tuple-element.54) | copy-start | bytes 24580
  173.8 12.7 %copy-start.15 = (f32[1,2048]{1,0:T(1,128)S(1)}, f32[1,2048]{1,0:T(1,128)}, u32[]{:S(2)}) copy-start(f32[1,2048]{1,0:T(1,128)} %get-tuple-element.55) | copy-start | bytes 24580
  173.8 12.7 %copy-start.16 = (f32[1,2048]{1,0:T(1,128)S(1)}, f32[1,2048]{1,0:T(1,128)}, u32[]{:S(2)}) copy-start(f32[1,2048]{1,0:T(1,128)} %get-tuple-element.56) | copy-start | bytes 24580
  173.8 12.7 %copy-start.17 = (f32[1,2048]{1,0:T(1,128)S(1)}, f32[1,2048]{1,0:T(1,128)}, u32[]{:S(2)}) copy-start(f32[1,2048]{1,0:T(1,128)} %get-tuple-element.57) | copy-start | bytes 24580
  173.8 12.7 %copy-start.18 = (f32[1,2048]{1,0:T(1,128)S(1)}, f32[1,2048]{1,0:T(1,128)}, u32[]{:S(2)}) copy-start(f32[1,2048]{1,0:T(1,128)} %get-tuple-element.58) | copy-start | bytes 24580
  173.8 12.7 %copy-start.19 = (f32[1,2048]{1,0:T(1,128)S(1)}, f32[1,2048]{1,0:T(1,128)}, u32[]{:S(2)}) copy-start(f32[1,2048]{1,0:T(1,128)} %get-tuple-element.59) | copy-start | bytes 24580
  173.8 12.7 %copy-start.20 = (f32[1,2048]{1,0:T(1,128)S(1)}, f32[1,2048]{1,0:T(1,128)}, u32[]{:S(2)}) copy-start(f32[1,2048]{1,0:T(1,128)} %get-tuple-element.60) | copy-start | bytes 24580
  173.8 12.7 %copy-start.21 = (f32[1,2048]{1,0:T(1,128)S(1)}, f32[1,2048]{1,0:T(1,128)}, u32[]{:S(2)}) copy-start(f32[1,2048]{1,0:T(1,128)} %get-tuple-element.61) | copy-start | bytes 24580
  173.9 12.7 %copy-start.22 = (f32[1,2048]{1,0:T(1,128)S(1)}, f32[1,2048]{1,0:T(1,128)}, u32[]{:S(2)}) copy-start(f32[1,2048]{1,0:T(1,128)} %get-tuple-element.62) | copy-start | bytes 24580
  173.9 12.7 %copy-start.23 = (f32[1,2048]{1,0:T(1,128)S(1)}, f32[1,2048]{1,0:T(1,128)}, u32[]{:S(2)}) copy-start(f32[1,2048]{1,0:T(1,128)} %get-tuple-element.63) | copy-start | bytes 24580
  173.9 12.7 %copy-start.24 = (f32[1,2048]{1,0:T(1,128)S(1)}, f32[1,2048]{1,0:T(1,128)}, u32[]{:S(2)}) copy-start(f32[1,2048]{1,0:T(1,128)} %get-tuple-element.64) | copy-start | bytes 24580
  175.3 10.0 %collective-permute-start.17 = (bf16[2,15,2048]{2,1,0:T(8,128)(2,1)S(1)}, bf16[2,15,2048]{2,1,0:T(8,128)(2,1)S(1)}, u32[]{:S(2)}, u32[]{:S(2)}) collective-permute-start(bf16[2,15,2048]{2,1,0:T(8,128)(2,1)S(1)} %get-tuple-element.38), channel_id=1, source_target_pairs={{1,0},{2,1},{3,2},{4,3},{5,4},{6,5},{7,6},{8,7},{9,8},{10,9},{11,1... | collective-permute-start | bytes 368648 | tf_op jit(solution)/shard_map/ppermute | solution.py:36
  176.6 9.7 %collective-permute-start.18 = (bf16[2,15,2048]{2,1,0:T(8,128)(2,1)S(1)}, bf16[2,15,2048]{2,1,0:T(8,128)(2,1)S(1)}, u32[]{:S(2)}, u32[]{:S(2)}) collective-permute-start(bf16[2,15,2048]{2,1,0:T(8,128)(2,1)S(1)} %get-tuple-element.39), channel_id=1, source_target_pairs={{0,1},{1,2},{2,3},{3,4},{4,5},{5,6},{6,7},{7,8},{8,9},{9,10},{10,1... | collective-permute-start | bytes 368648 | tf_op jit(solution)/shard_map/ppermute | solution.py:33
  (12 other events, 125.2 us)
Sparse Core Ops, SparseCore 0:
  160.0 57.2 reduce-scatter.4
  222.0 176.3 reduce-scatter.2
